TPU v7x, 32 devices: a whole 2x2x4 slice. The times are simulated.
32 devices in a mesh: dp: 4 (over y, x), tile: 8 (over z, core).
Axes of the slice: x: 2, y: 2, z: 4, core: 2. Of those that a mesh axis runs over, the one named last changes fastest.
Arguments:
- features: bfloat16 [4, 8, 512, 1280], P('dp', 'tile'), may hold values from -6 to 6
- visible: int32 [4, 8, 512], P('dp', 'tile'), may hold values from 0 to 1, as said below
- positions: int32 [4, 8, 512], P('dp', 'tile'), may hold values from 0 to 511, each once within a row
- cotangent: bfloat16 [4, 8, 512, 512], P('dp', 'tile'), may hold values from -6 to 6
- mlp_gain: float32 [1280], replicated, may hold values from 0.1 to 1.9
- mlp_bias: float32 [1280], replicated, may hold values from -3 to 3
- fc1_weight: bfloat16 [1280, 2560], replicated, may hold values from -0.15625 to 0.15625
- fc1_bias: float32 [2560], replicated, may hold values from -3 to 3
- fc2_weight: bfloat16 [2560, 1280], replicated, may hold values from -0.125 to 0.125
- fc2_bias: float32 [1280], replicated, may hold values from -3 to 3
- encoder_gain: float32 [1280], replicated, may hold values from 0.1 to 1.9
- encoder_bias: float32 [1280], replicated, may hold values from -3 to 3
- embed_weight: bfloat16 [1280, 512], replicated, may hold values from -0.15625 to 0.15625
- embed_bias: float32 [512], replicated, may hold values from -3 to 3
- mask_token: float32 [512], replicated, may hold values from -4 to 4
- position_table: bfloat16 [512, 512], replicated, may hold values from -4 to 4
- decoder_gain: float32 [512], replicated, may hold values from 0.1 to 1.9
- decoder_bias: float32 [512], replicated, may hold values from -3 to 3
Outputs:
- feature_grad: bfloat16 [4, 8, 512, 1280], P('dp', 'tile')
- decoded: bfloat16 [4, 8, 512, 512], P('dp', 'tile')
- fc1_grad: float32 [1280, 2560], P('tile')
- fc2_grad: float32 [2560, 1280], P('tile')
Inputs may be any that keep to these rules, and one draw needn't show every extreme that they name: In each scene (all 8 chips of one index of the first dimension) exactly 1024 patches are visible; each chip has at most 256 visible patches, and in every scene one chip has exactly 256. Each chip's position ids are a permutation of its 512 positions.
All inputs are finite; a program needn't handle non-finite values.
Results may differ from a plain program's by a relative error of at most 0.007.
Values may be sent and summed in bfloat16 or wider, within the bound.
A program may use at most 128 MiB of HBM per device.

v0:
```python
import jax
import jax.numpy as jnp
from jax import lax
from jax.sharding import PartitionSpec as P

epsilon = 1e-06


def layer_norm(values, norm_gain, norm_bias):
    row_mean = jnp.mean(values, axis=-1, keepdims=True)
    centred = values - row_mean
    variance = jnp.mean(centred * centred, axis=-1, keepdims=True)
    inv_std = lax.rsqrt(variance + epsilon)
    scaled = centred * inv_std
    return (scaled * norm_gain + norm_bias, scaled, inv_std)


def norm_back(upstream, scaled, inv_std):
    mean_up = jnp.mean(upstream, axis=-1, keepdims=True)
    mean_cross = jnp.mean(upstream * scaled, axis=-1, keepdims=True)
    return inv_std * (upstream - mean_up - scaled * mean_cross)


def gelu_parts(pre_act):
    normal_cdf = 0.5 * (1.0 + lax.erf(pre_act * 0.7071067811865476))
    density = jnp.exp(-0.5 * pre_act * pre_act) * 0.3989422804014327
    return (pre_act * normal_cdf, normal_cdf + pre_act * density)


def encode(enc_input, enc_params):
    (
        mlp_gain,
        mlp_bias,
        fc1_weight,
        fc1_bias,
        fc2_weight,
        fc2_bias,
        encoder_gain,
        encoder_bias,
        embed_weight,
        embed_bias,
    ) = enc_params
    rows_in = enc_input.astype(jnp.float32)
    mlp_in, mlp_scaled, mlp_inv = layer_norm(rows_in, mlp_gain, mlp_bias)
    mlp_in = mlp_in.astype(jnp.bfloat16)
    pre_act = jnp.dot(mlp_in, fc1_weight, preferred_element_type=jnp.float32) + fc1_bias
    activation, slope = gelu_parts(pre_act)
    hidden = activation.astype(jnp.bfloat16)
    encoded = rows_in + jnp.dot(hidden, fc2_weight, preferred_element_type=jnp.float32) + fc2_bias
    normed, enc_scaled, enc_inv = layer_norm(encoded, encoder_gain, encoder_bias)
    normed = normed.astype(jnp.bfloat16)
    projected = (
        jnp.dot(normed, embed_weight, preferred_element_type=jnp.float32) + embed_bias
    ).astype(jnp.bfloat16)
    saved = (mlp_in, mlp_scaled, mlp_inv, slope, hidden, enc_scaled, enc_inv)
    return (saved, projected)


def encode_back(saved, grad_compact, enc_params):
    (
        mlp_gain,
        mlp_bias,
        fc1_weight,
        fc1_bias,
        fc2_weight,
        fc2_bias,
        encoder_gain,
        encoder_bias,
        embed_weight,
        embed_bias,
    ) = enc_params
    mlp_in, mlp_scaled, mlp_inv, slope, hidden, enc_scaled, enc_inv = saved
    grad_normed = jnp.dot(grad_compact, embed_weight.T, preferred_element_type=jnp.float32)
    grad_encoded = norm_back(grad_normed * encoder_gain, enc_scaled, enc_inv).astype(jnp.bfloat16)
    grad_hidden = jnp.dot(grad_encoded, fc2_weight.T, preferred_element_type=jnp.float32)
    grad_pre = (grad_hidden * slope).astype(jnp.bfloat16)
    grad_mlp_in = jnp.dot(grad_pre, fc1_weight.T, preferred_element_type=jnp.float32)
    grad_feats = (
        grad_encoded.astype(jnp.float32) + norm_back(grad_mlp_in * mlp_gain, mlp_scaled, mlp_inv)
    ).astype(jnp.bfloat16)
    fc1_term = jnp.dot(mlp_in.T, grad_pre, preferred_element_type=jnp.float32)
    fc2_term = jnp.dot(hidden.T, grad_encoded, preferred_element_type=jnp.float32)
    return (fc1_term, fc2_term, grad_feats)


def decoder_pass(
    projected_rows,
    keep_rows,
    position_ids,
    upstream,
    position_table,
    mask_token,
    decoder_gain,
    decoder_bias,
):
    table_ids = jnp.arange(position_table.shape[0], dtype=jnp.int32)[None, :]
    pick = (position_ids[:, None] == table_ids).astype(jnp.bfloat16)
    placed = jnp.dot(pick, position_table, preferred_element_type=jnp.float32)
    dec_input = jnp.where(keep_rows, projected_rows, mask_token) + placed
    decoded, dec_scaled, dec_inv = layer_norm(dec_input, decoder_gain, decoder_bias)
    grad_input = norm_back(upstream.astype(jnp.float32) * decoder_gain, dec_scaled, dec_inv)
    grad_projected = jnp.where(keep_rows, grad_input, 0.0).astype(jnp.bfloat16)
    return (decoded.astype(jnp.bfloat16), grad_projected)


def shards(
    features,
    visible,
    positions,
    cotangent,
    mlp_gain,
    mlp_bias,
    fc1_weight,
    fc1_bias,
    fc2_weight,
    fc2_bias,
    encoder_gain,
    encoder_bias,
    embed_weight,
    embed_bias,
    mask_token,
    position_table,
    decoder_gain,
    decoder_bias,
):
    patch_count = features.shape[2]
    model_width = features.shape[3]
    dec_width = embed_weight.shape[1]
    most_rows = patch_count // 2
    flags = visible.reshape(patch_count)
    row_data = features.reshape(patch_count, model_width)
    keep_rows = (flags > 0)[:, None]
    upstream = cotangent.reshape(patch_count, dec_width)
    ids = jnp.arange(patch_count, dtype=jnp.int32)
    row_rank = jnp.sum(jnp.where(ids[None, :] < ids[:, None], flags[None, :], 0), axis=1)
    slots = jnp.arange(most_rows, dtype=jnp.int32)
    target = jnp.where(flags > 0, row_rank, -1)
    gather = (slots[:, None] == target[None, :]).astype(jnp.bfloat16)
    scatter = (target[:, None] == slots[None, :]).astype(jnp.bfloat16)
    enc_params = (
        mlp_gain,
        mlp_bias,
        fc1_weight,
        fc1_bias,
        fc2_weight,
        fc2_bias,
        encoder_gain,
        encoder_bias,
        embed_weight,
        embed_bias,
    )
    decoder_args = (position_table, mask_token, decoder_gain, decoder_bias)
    enc_input = jnp.dot(gather, row_data, preferred_element_type=jnp.bfloat16)
    saved, projected = encode(enc_input, enc_params)
    projected_rows = jnp.dot(scatter, projected, preferred_element_type=jnp.float32)
    decoded, grad_projected = decoder_pass(
        projected_rows, keep_rows, positions.reshape(-1), upstream, *decoder_args
    )
    grad_compact = jnp.dot(gather, grad_projected, preferred_element_type=jnp.bfloat16)
    fc1_term, fc2_term, grad_feats = encode_back(saved, grad_compact, enc_params)
    grad_rows = jnp.dot(scatter, grad_feats, preferred_element_type=jnp.bfloat16)
    device_total = lax.axis_size("dp") * lax.axis_size("tile")
    totals = []
    for term in (fc1_term, fc2_term):
        share = lax.psum_scatter(term.astype(jnp.bfloat16), "tile", scatter_dimension=0, tiled=True)
        totals.append(lax.psum(share, "dp").astype(jnp.float32) / device_total)
    fc1_grad, fc2_grad = totals
    feature_grad = grad_rows.reshape(features.shape)
    decoded_out = decoded.reshape(cotangent.shape)
    return (feature_grad, decoded_out, fc1_grad, fc2_grad)


def solution(mesh):
    return jax.shard_map(
        shards,
        mesh=mesh,
        in_specs=(
            P("dp", "tile", None, None),
            P("dp", "tile", None),
            P("dp", "tile", None),
            P("dp", "tile", None, None),
            P(),
            P(),
            P(),
            P(),
            P(),
            P(),
            P(),
            P(),
            P(),
            P(),
            P(),
            P(),
            P(),
            P(),
        ),
        out_specs=(
            P("dp", "tile", None, None),
            P("dp", "tile", None, None),
            P("tile", None),
            P("tile", None),
        ),
        check_vma=False,
    )
```

profile of v0, /device:TPU:0, one launch (start us, length us, event | category | flops | bytes accessed | tf_op | source)
XLA Modules:
  0.0 269.7 jit_solution(12920631367889845395)
XLA Ops:
  7.2 0.0 copy-start
  7.2 0.0 reduce-scatter.3.cloned.1.call-start
  7.2 0.9 select_reduce_fusion
  8.1 0.7 broadcast_select_fusion
  8.8 1.9 fusion.60
  10.8 0.0 copy-start.9
  10.8 0.0 slice-start
  10.8 0.3 multiply_reduce_fusion.3
  11.1 0.4 copy-done.8
  11.4 0.0 copy-done.9
  11.5 0.0 copy-done.13
  11.5 5.2 %convolution_add_fusion = f32[256,2560]{1,0:T(8,128)S(1)} fusion(bf16[1280,2560]{1,0:T(8,128)(2,1)} %param.24, f32[2560]{0:T(1024)S(1)} %copy-done.13, f32[256,1280]{1,0:T(8,128)S(1)} %get-tuple-element.24, f32[1280]{0:T(1024)S(1)} %copy-done.8, f32[1280]{0:T(1024)S(1)} %copy-done.9, f32[256]{0:T(256)S(1)} %add_rsqrt_fusion.2, ...), kind=kOutput, calls=%fused_computation.3 | convolution fusion | flops 1680015360 | bytes 10508288 | tf_op jit(solution)/shard_map/dot_general | solution.py:46
  16.7 2.2 fusion.61
  18.9 0.0 copy-start.15
  18.9 0.0 copy-start.16
  19.0 1.0 copy-done.4
  20.0 0.3 multiply_reduce_fusion.2
  20.3 0.0 copy-start.7
  20.3 0.0 copy-start.10
  20.3 3.2 %convolution_select_fusion = f32[512,512]{0,1:T(8,128)} fusion(bf16[1280,512]{1,0:T(8,128)(2,1)S(1)} %copy-done, f32[256,1280]{1,0:T(8,128)} %copy-done.4, f32[1280]{0:T(1024)S(1)} %copy-done.15, f32[1280]{0:T(1024)S(1)} %copy-done.16, f32[256]{0:T(256)S(1)} %add_rsqrt_fusion.1, f32[256]{0:T(256)S(1)} %broadcast_multiply_fusion.7, f32[512]{0:T(512)S(1)} %copy-done.17, ...), kind=kOutput, calls=%fused_computation.21 | convolution fusion | flops 472055808 | bytes 3688960 | tf_op jit(solution)/shard_map/dot_general | solution.py:155
  23.6 1.9 fusion.62
  25.5 0.0 copy-start.1
  25.5 0.0 copy-start.11
  25.5 0.9 copy-done.1
  26.4 0.2 multiply_reduce_fusion.4
  26.6 1.3 copy.24
  27.9 2.4 fusion.12
  30.3 3.7 %fusion.59 = (f32[256]{0:T(256)S(1)}, f32[256]{0:T(256)S(1)}, f32[256,1280]{1,0:T(8,128)}) fusion(f32[256]{0:T(256)S(1)} %add_rsqrt_fusion.1, f32[256,1280]{1,0:T(8,128)} %copy-done.4, f32[256]{0:T(256)S(1)} %broadcast_multiply_fusion.7, f32[1280]{0:T(1024)S(1)} %copy-done.16, bf16[1280,512]{1,0:T(8,128)(2,1)S(1)} %copy-done, f32[512,512]{0,1:T(8,128)} %copy-done.1, ...), kind=kOutput, calls=%fused_computation.92 | convolution fusion | flops 474480128 | bytes 5527040 | tf_op jit(solution)/shard_map/dot_general | solution.py:73
  34.1 2.2 multiply_convert_fusion.1
  36.3 0.3 copy-done.3
  36.6 5.0 %fusion = bf16[256,2560]{1,0:T(8,128)(2,1)S(1)} fusion(bf16[256,1280]{1,0:T(8,128)(2,1)S(1)} %multiply_convert_fusion.1, bf16[2560,1280]{1,0:T(8,128)(2,1)} %param.26, f32[256,2560]{1,0:T(8,128)S(1)} %copy-done.3), kind=kOutput, calls=%fused_computation.5 | convolution fusion | flops 1684275200 | bytes 11141120 | tf_op jit(solution)/shard_map/dot_general | solution.py:75
  41.6 0.0 copy-start.5
  41.7 1.0 copy-done.5
  42.7 4.8 %convolution_convert_fusion.1 = bf16[1280,2560]{1,0:T(8,128)(2,1)} fusion(bf16[256,2560]{1,0:T(8,128)(2,1)S(1)} %fusion, f32[256,1280]{1,0:T(8,128)S(1)} %get-tuple-element.24, f32[1280]{0:T(1024)S(1)} %copy-done.8, f32[1280]{0:T(1024)S(1)} %copy-done.9, f32[256]{0:T(256)S(1)} %add_rsqrt_fusion.2, f32[256]{0:T(256)S(1)} %broadcast_multiply_fusion.8), kind=kOutput, calls=%fused_computation.1 | convolution fusion | flops 1682636800 | bytes 9187328 | tf_op jit(solution)/shard_map/dot_general | solution.py:81
  47.5 0.0 reduce-scatter.3.cloned.1.call-update
  47.5 0.2 reduce-scatter.5.cloned.1.call-start
  47.7 6.7 %convolution_convert_fusion = bf16[2560,1280]{1,0:T(8,128)(2,1)} fusion(bf16[256,1280]{1,0:T(8,128)(2,1)S(1)} %multiply_convert_fusion.1, f32[256,2560]{1,0:T(8,128)} %copy-done.2), kind=kOutput, calls=%fused_computation | convolution fusion | flops 1684275200 | bytes 9830400 | tf_op jit(solution)/shard_map/dot_general | solution.py:82
  54.4 0.0 reduce-scatter.5.cloned.1.call-update
  54.5 0.0 all-reduce.3.cloned.1.call-start
  54.5 68.1 %reduce-scatter.3.cloned.1.call-done = bf16[160,2560]{1,0:T(8,128)(2,1)} async-done(((bf16[1280,2560]{1,0:T(8,128)(2,1)}), bf16[160,2560]{1,0:T(8,128)(2,1)}) %reduce-scatter.3.cloned.1.call-update) | async-done | bytes 819216 | tf_op jit(solution)/shard_map/reduce_scatter | solution.py:165
  122.6 73.0 %reduce-scatter.5.cloned.1.call-done = bf16[320,1280]{1,0:T(8,128)(2,1)} async-done(((bf16[2560,1280]{1,0:T(8,128)(2,1)}), bf16[320,1280]{1,0:T(8,128)(2,1)}) %reduce-scatter.5.cloned.1.call-update) | async-done | bytes 819216 | tf_op jit(solution)/shard_map/reduce_scatter | solution.py:165
  195.6 0.0 all-reduce.3.cloned.1.call-update
  195.6 2.0 copy.25
  197.7 5.3 %fusion.58 = (f32[256]{0:T(256)S(1)}, f32[256]{0:T(256)S(1)}, f32[256,1280]{1,0:T(8,128)S(1)}) fusion(f32[256]{0:T(256)S(1)} %add_rsqrt_fusion.2, f32[256,1280]{1,0:T(8,128)S(1)} %get-tuple-element.24, f32[256]{0:T(256)S(1)} %broadcast_multiply_fusion.8, f32[1280]{0:T(1024)S(1)} %copy-done.9, bf16[256,2560]{1,0:T(8,128)(2,1)} %copy-done.5, ...), kind=kOutput, calls=%fused_computation.91 | convolution fusion | flops 1679687168 | bytes 10494976 | tf_op jit(solution)/shard_map/dot_general | solution.py:77
  203.0 2.0 convolution_bitcast_fusion
  205.0 54.3 %all-reduce.3.cloned.1.call-done = (bf16[160,2560]{1,0:T(8,128)(2,1)}, bf16[320,1280]{1,0:T(8,128)(2,1)}) async-done(((bf16[160,2560]{1,0:T(8,128)(2,1)}, bf16[320,1280]{1,0:T(8,128)(2,1)}), (bf16[160,2560]{1,0:T(8,128)(2,1)}, bf16[320,1280]{1,0:T(8,128)(2,1)})) %all-reduce.3.cloned.1.call-update) | async-done | bytes 1638416 | tf_op jit(solution)/shard_map/psum | solution.py:166
  259.3 2.5 convert_multiply_fusion
  261.8 1.3 convert_multiply_fusion.1
  (37 shorter events, 0.1 us)
Async XLA Ops:
  7.2 13.1 %copy-start = (bf16[1280,512]{1,0:T(8,128)(2,1)S(1)}, bf16[1280,512]{1,0:T(8,128)(2,1)}, u32[]{:S(2)}) copy-start(bf16[1280,512]{1,0:T(8,128)(2,1)} %param.30) | copy-start | bytes 3932164
  7.2 115.5 %reduce-scatter.3.cloned.1.call-start = ((), (), s32[]{:S(2)}) async-start(), calls=%async_computation.2 | async-start | bytes 7372800 | tf_op jit(solution)/shard_map/reduce_scatter | solution.py:165
  10.7 0.7 copy-start.8
  10.8 0.7 copy-start.9
  10.8 0.7 copy-start.13
  10.8 5.9 %slice-start = ((s8[6553600]{0:T(1024)(128)(4,1)}), s8[4194304]{0:T(1024)(128)(4,1)S(1)}, s32[]{:S(2)}) async-start(s8[6553600]{0:T(1024)(128)(4,1)} %bitcast.36), calls=%async_computation.5 | async-start | bytes 8388608
  11.5 5.2 %slice-start.1 = ((s8[6553600]{0:T(1024)(128)(4,1)}), s8[2359296]{0:T(1024)(128)(4,1)S(1)}, s32[]{:S(2)}) async-start(s8[6553600]{0:T(1024)(128)(4,1)} %bitcast.36), calls=%async_computation.6 | async-start | bytes 4718592
  11.5 5.2 %copy-start.14 = (f32[1280]{0:T(1024)S(1)}, f32[1280]{0:T(1024)}, u32[]{:S(2)}) copy-start(f32[1280]{0:T(1024)} %param.27) | copy-start | bytes 15364
  16.7 2.2 copy-start.2
  18.9 1.1 copy-start.4
  18.9 1.3 copy-start.15
  18.9 1.3 copy-start.16
  19.0 1.3 copy-start.17
  19.0 1.3 copy-start.18
  20.3 3.3 %copy-start.7 = (bf16[512,512]{1,0:T(8,128)(2,1)S(1)}, bf16[512,512]{1,0:T(8,128)(2,1)}, u32[]{:S(2)}) copy-start(bf16[512,512]{1,0:T(8,128)(2,1)} %param.33) | copy-start | bytes 1572868
  20.3 3.2 %copy-start.10 = (s32[1,1,512]{2,1,0:T(1,128)S(1)}, s32[1,1,512]{2,1,0:T(1,128)}, u32[]{:S(2)}) copy-start(s32[1,1,512]{2,1,0:T(1,128)} %param.20) | copy-start | bytes 6148
  25.5 1.0 copy-start.1
  25.5 2.4 copy-start.11
  25.5 2.4 copy-start.12
  34.1 2.5 copy-start.3
  41.6 1.1 copy-start.5
  47.5 148.1 %reduce-scatter.5.cloned.1.call-start = ((), (), s32[]{:S(2)}) async-start(), calls=%async_computation.3 | async-start | bytes 7372800 | tf_op jit(solution)/shard_map/reduce_scatter | solution.py:165
  54.5 204.9 %all-reduce.3.cloned.1.call-start = ((), (), s32[]{:S(2)}) async-start(), calls=%async_computation.4 | async-start | bytes 3276800 | tf_op jit(solution)/shard_map/psum | solution.py:166
  259.3 2.5 copy-start.6
Sparse Core Ops, SparseCore 0:
  47.6 74.9 reduce-scatter.2
  125.0 70.6 reduce-scatter.4
  198.8 60.5 all-reduce.2
where the time goes:
time: 270 us
  waiting for transfers between devices  195 us (72%)
  matrix products  41.9 us (16%)
  between operations  14.1 us (5%)
  other arithmetic  10.9 us (4%)
  local copies, waits for them, and re-layouts  7.04 us (3%)
    reduce_scatter x2, waiting for transfers between devices, shards(): lax.psum_scatter(term.astype(jnp.bfloat16), 'tile', scatter_dimension=0,...  141 us
    psum x1, waiting for transfers between devices, shards(): totals.append(lax.psum(share, 'dp').astype(jnp.float32) / device_total)  54.3 us
    unnamed x44, local copies, waits for them, and re-layouts  7.04 us
    dot_general x1, matrix products, encode_back(): jnp.dot(hidden.T, grad_encoded, preferred_element_type=jnp.float32)  6.71 us
  transfers between devices with their start and end apart: 3, of which 3 were waited for; matrix products, arithmetic and copies ran while one was open for 6% of the time, Pallas kernels for 0%

commit v1 on v0

--- a/solution.py
+++ b/solution.py
@@ -163,7 +163,11 @@
     totals = []
     for term in (fc1_term, fc2_term):
         share = lax.psum_scatter(term.astype(jnp.bfloat16), "tile", scatter_dimension=0, tiled=True)
-        totals.append(lax.psum(share, "dp").astype(jnp.float32) / device_total)
+
+        def view_lead(base_x):
+            return jnp.sum(lax.all_gather(base_x, axis_name="dp"), axis=0)
+
+        totals.append(view_lead(share).astype(jnp.float32) / device_total)
     fc1_grad, fc2_grad = totals
     feature_grad = grad_rows.reshape(features.shape)
     decoded_out = decoded.reshape(cotangent.shape)

time: 270 us -> 290 us (1.074)
  waiting for transfers between devices: 195 us -> 213 us
    all_gather x0 -> x2, waiting for transfers between devices: none -> 78.6 us  [view_lead(): return jnp.sum(lax.all_gather(base_x, axis_name='dp'), axis=0)]
    psum x1 -> x0, waiting for transfers between devices: 54.3 us -> none  [shards(): totals.append(lax.psum(share, 'dp').astype(jnp.float32) / device_total)]
    reduce_scatter x2, waiting for transfers between devices: 141 us -> 134 us  [shards(): lax.psum_scatter(term.astype(jnp.bfloat16), 'tile', scatter_dimension=0,...]
    reduce_sum x0 -> x2, other arithmetic: none -> 5.3 us  [view_lead(): return jnp.sum(lax.all_gather(base_x, axis_name='dp'), axis=0)]
    unnamed x44 -> x40, local copies, waits for them, and re-layouts: 7.04 us -> 6.1 us
  transfers between devices with their start and end apart: 3 -> 4, of which waited for: 3 -> 4; matrix products, arithmetic and copies ran while one was open for 6% -> 9% of each run, Pallas kernels for 0% -> 0%
where the time goes in v1:
time: 290 us; the launch traced here: 289 us
  waiting for transfers between devices  213 us (73%)
  matrix products  42.2 us (15%)
  between operations  14.1 us (5%)
  other arithmetic  13.7 us (5%)
  local copies, waits for them, and re-layouts  6.1 us (2%)
    reduce_scatter x2, waiting for transfers between devices, shards(): lax.psum_scatter(term.astype(jnp.bfloat16), 'tile', scatter_dimension=0,...  134 us
    all_gather x2, waiting for transfers between devices, view_lead(): return jnp.sum(lax.all_gather(base_x, axis_name='dp'), axis=0)  78.6 us
    dot_general x1, matrix products, encode_back(): jnp.dot(grad_encoded, fc2_weight.T, preferred_element_type=jnp.float32)  7.8 us
    unnamed x40, local copies, waits for them, and re-layouts  6.1 us
  transfers between devices with their start and end apart: 4, of which 4 were waited for; matrix products, arithmetic and copies ran while one was open for 9% of the time, Pallas kernels for 0%

profile of v1, /device:TPU:0, one launch (start us, length us, event | category | flops | bytes accessed | tf_op | source)
XLA Modules:
  0.0 289.2 jit_solution(1139976037994404412)
XLA Ops:
  7.2 0.0 copy-start
  7.2 0.0 reduce-scatter.5.cloned.1.call-start
  7.2 0.9 select_reduce_fusion
  8.1 0.7 broadcast_select_fusion
  8.8 1.3 copy.24
  10.1 1.9 fusion.60
  12.0 0.0 copy-start.7
  12.1 0.0 slice-start
  12.1 0.3 multiply_reduce_fusion.3
  12.4 0.4 copy-done.6
  12.7 0.0 copy-done.7
  12.7 0.0 copy-done.11
  12.8 5.2 %convolution_add_fusion = f32[256,2560]{1,0:T(8,128)S(1)} fusion(bf16[1280,2560]{1,0:T(8,128)(2,1)} %param.24, f32[2560]{0:T(1024)S(1)} %copy-done.11, f32[256,1280]{1,0:T(8,128)S(1)} %get-tuple-element.22, f32[1280]{0:T(1024)S(1)} %copy-done.6, f32[1280]{0:T(1024)S(1)} %copy-done.7, f32[256]{0:T(256)S(1)} %add_rsqrt_fusion.2, ...), kind=kOutput, calls=%fused_computation.3 | convolution fusion | flops 1680015360 | bytes 10508288 | tf_op jit(solution)/shard_map/dot_general | solution.py:46
  18.0 2.1 fusion.61
  20.2 0.0 copy-start.14
  20.2 0.0 copy-start.15
  20.2 1.0 copy-done.4
  21.2 0.3 multiply_reduce_fusion.2
  21.5 3.2 %convolution_select_fusion = f32[512,512]{0,1:T(8,128)} fusion(bf16[1280,512]{1,0:T(8,128)(2,1)S(1)} %copy-done, f32[256,1280]{1,0:T(8,128)} %copy-done.4, f32[1280]{0:T(1024)S(1)} %copy-done.13, f32[1280]{0:T(1024)S(1)} %copy-done.14, f32[256]{0:T(256)S(1)} %add_rsqrt_fusion.1, f32[256]{0:T(256)S(1)} %broadcast_multiply_fusion.7, f32[512]{0:T(512)S(1)} %copy-done.15, ...), kind=kOutput, calls=%fused_computation.21 | convolution fusion | flops 472055808 | bytes 3688960 | tf_op jit(solution)/shard_map/dot_general | solution.py:155
  24.7 2.1 fusion.62
  26.8 0.2 multiply_reduce_fusion.4
  27.0 1.2 fusion.12
  28.2 3.7 %fusion.59 = (f32[256]{0:T(256)S(1)}, f32[256]{0:T(256)S(1)}, f32[256,1280]{1,0:T(8,128)}) fusion(f32[256]{0:T(256)S(1)} %add_rsqrt_fusion.1, f32[256,1280]{1,0:T(8,128)} %copy-done.4, f32[256]{0:T(256)S(1)} %broadcast_multiply_fusion.7, f32[1280]{0:T(1024)S(1)} %copy-done.14, bf16[1280,512]{1,0:T(8,128)(2,1)S(1)} %copy-done, f32[512,512]{0,1:T(8,128)} %copy-done.1, ...), kind=kOutput, calls=%fused_computation.92 | convolution fusion | flops 474480128 | bytes 5527040 | tf_op jit(solution)/shard_map/dot_general | solution.py:73
  32.0 2.2 multiply_convert_fusion.1
  34.2 0.3 copy-done.3
  34.5 4.2 %convolution_convert_fusion = bf16[2560,1280]{1,0:T(8,128)(2,1)} fusion(bf16[256,1280]{1,0:T(8,128)(2,1)S(1)} %multiply_convert_fusion.1, f32[256,2560]{1,0:T(8,128)S(1)} %copy-done.3), kind=kOutput, calls=%fused_computation | convolution fusion | flops 1684275200 | bytes 9830400 | tf_op jit(solution)/shard_map/dot_general | solution.py:82
  38.7 0.0 reduce-scatter.5.cloned.1.call-update
  38.7 0.2 reduce-scatter.3.cloned.1.call-start
  38.9 7.8 %fusion = bf16[256,2560]{1,0:T(8,128)(2,1)S(1)} fusion(bf16[256,1280]{1,0:T(8,128)(2,1)S(1)} %multiply_convert_fusion.1, bf16[2560,1280]{1,0:T(8,128)(2,1)} %param.26, f32[256,2560]{1,0:T(8,128)} %copy-done.2), kind=kOutput, calls=%fused_computation.5 | convolution fusion | flops 1684275200 | bytes 11141120 | tf_op jit(solution)/shard_map/dot_general | solution.py:75
  46.7 0.0 copy-start.5
  46.7 1.0 copy-done.5
  47.8 4.7 %convolution_convert_fusion.1 = bf16[1280,2560]{1,0:T(8,128)(2,1)} fusion(bf16[256,2560]{1,0:T(8,128)(2,1)S(1)} %fusion, f32[256,1280]{1,0:T(8,128)S(1)} %get-tuple-element.22, f32[1280]{0:T(1024)S(1)} %copy-done.6, f32[1280]{0:T(1024)S(1)} %copy-done.7, f32[256]{0:T(256)S(1)} %add_rsqrt_fusion.2, f32[256]{0:T(256)S(1)} %broadcast_multiply_fusion.8), kind=kOutput, calls=%fused_computation.1 | convolution fusion | flops 1682636800 | bytes 9187328 | tf_op jit(solution)/shard_map/dot_general | solution.py:81
  52.5 0.0 reduce-scatter.3.cloned.1.call-update
  52.6 0.0 all-gather.7.cloned.1.call-start
  52.6 61.2 %reduce-scatter.5.cloned.1.call-done = bf16[320,1280]{1,0:T(8,128)(2,1)} async-done(((bf16[2560,1280]{1,0:T(8,128)(2,1)}), bf16[320,1280]{1,0:T(8,128)(2,1)}) %reduce-scatter.5.cloned.1.call-update) | async-done | bytes 819216 | tf_op jit(solution)/shard_map/reduce_scatter | solution.py:165
  113.8 0.0 all-gather.7.cloned.1.call-update
  113.8 0.0 all-gather.5.cloned.1.call-start
  113.9 72.9 %reduce-scatter.3.cloned.1.call-done = bf16[160,2560]{1,0:T(8,128)(2,1)} async-done(((bf16[1280,2560]{1,0:T(8,128)(2,1)}), bf16[160,2560]{1,0:T(8,128)(2,1)}) %reduce-scatter.3.cloned.1.call-update) | async-done | bytes 819216 | tf_op jit(solution)/shard_map/reduce_scatter | solution.py:165
  186.8 0.0 all-gather.5.cloned.1.call-update
  186.8 2.0 copy.25
  188.9 5.3 %fusion.58 = (f32[256]{0:T(256)S(1)}, f32[256]{0:T(256)S(1)}, f32[256,1280]{1,0:T(8,128)S(1)}) fusion(f32[256]{0:T(256)S(1)} %add_rsqrt_fusion.2, f32[256,1280]{1,0:T(8,128)S(1)} %get-tuple-element.22, f32[256]{0:T(256)S(1)} %broadcast_multiply_fusion.8, f32[1280]{0:T(1024)S(1)} %copy-done.7, bf16[256,2560]{1,0:T(8,128)(2,1)} %copy-done.5, ...), kind=kOutput, calls=%fused_computation.91 | convolution fusion | flops 1679687168 | bytes 10494976 | tf_op jit(solution)/shard_map/dot_general | solution.py:77
  194.2 2.0 convolution_bitcast_fusion
  196.1 36.0 %all-gather.7.cloned.1.call-done = bf16[1280,1280]{1,0:T(8,128)(2,1)} async-done(((bf16[320,1280]{1,0:T(8,128)(2,1)}), bf16[1280,1280]{1,0:T(8,128)(2,1)}) %all-gather.7.cloned.1.call-update) | async-done | bytes 3276816 | tf_op jit(solution)/shard_map/all_gather | solution.py:168
  232.1 2.8 reduce_sum.155
  234.9 1.3 convert_multiply_fusion
  236.2 42.7 %all-gather.5.cloned.1.call-done = bf16[640,2560]{1,0:T(8,128)(2,1)} async-done(((bf16[160,2560]{1,0:T(8,128)(2,1)}), bf16[640,2560]{1,0:T(8,128)(2,1)}) %all-gather.5.cloned.1.call-update) | async-done | bytes 3276816 | tf_op jit(solution)/shard_map/all_gather | solution.py:168
  278.9 2.5 reduce_sum.154
  281.4 1.3 convert_multiply_fusion.1
  (38 shorter events, 0.1 us)
Async XLA Ops:
  7.2 14.3 %copy-start = (bf16[1280,512]{1,0:T(8,128)(2,1)S(1)}, bf16[1280,512]{1,0:T(8,128)(2,1)}, u32[]{:S(2)}) copy-start(bf16[1280,512]{1,0:T(8,128)(2,1)} %param.30) | copy-start | bytes 3932164
  7.2 106.6 %reduce-scatter.5.cloned.1.call-start = ((), (), s32[]{:S(2)}) async-start(), calls=%async_computation.3 | async-start | bytes 7372800 | tf_op jit(solution)/shard_map/reduce_scatter | solution.py:165
  12.0 0.7 copy-start.6
  12.0 0.7 copy-start.7
  12.0 0.7 copy-start.11
  12.1 5.9 %slice-start = ((s8[6553600]{0:T(1024)(128)(4,1)}), s8[4194304]{0:T(1024)(128)(4,1)S(1)}, s32[]{:S(2)}) async-start(s8[6553600]{0:T(1024)(128)(4,1)} %bitcast.40), calls=%async_computation.6 | async-start | bytes 8388608
  12.8 5.2 %slice-start.1 = ((s8[6553600]{0:T(1024)(128)(4,1)}), s8[2359296]{0:T(1024)(128)(4,1)S(1)}, s32[]{:S(2)}) async-start(s8[6553600]{0:T(1024)(128)(4,1)} %bitcast.40), calls=%async_computation.7 | async-start | bytes 4718592
  12.8 5.2 %copy-start.12 = (f32[1280]{0:T(1024)S(1)}, f32[1280]{0:T(1024)}, u32[]{:S(2)}) copy-start(f32[1280]{0:T(1024)} %param.27) | copy-start | bytes 15364
  18.0 2.2 copy-start.2
  20.1 1.1 copy-start.4
  20.2 1.3 copy-start.13
  20.2 1.3 copy-start.14
  20.2 1.3 copy-start.15
  20.2 1.3 copy-start.16
  21.5 3.2 %copy-start.8 = (s32[1,1,512]{2,1,0:T(1,128)S(1)}, s32[1,1,512]{2,1,0:T(1,128)}, u32[]{:S(2)}) copy-start(s32[1,1,512]{2,1,0:T(1,128)} %param.20) | copy-start | bytes 6148
  24.7 2.3 copy-start.9
  24.7 2.3 copy-start.10
  26.8 1.4 copy-start.1
  32.0 2.5 copy-start.3
  38.7 148.1 %reduce-scatter.3.cloned.1.call-start = ((), (), s32[]{:S(2)}) async-start(), calls=%async_computation.2 | async-start | bytes 7372800 | tf_op jit(solution)/shard_map/reduce_scatter | solution.py:165
  46.7 1.1 copy-start.5
  52.6 179.5 %all-gather.7.cloned.1.call-start = ((), (), s32[]{:S(2)}) async-start(), calls=%async_computation.5 | async-start | bytes 4096000 | tf_op jit(solution)/shard_map/all_gather | solution.py:168
  113.8 165.1 %all-gather.5.cloned.1.call-start = ((), (), s32[]{:S(2)}) async-start(), calls=%async_computation.4 | async-start | bytes 4096000 | tf_op jit(solution)/shard_map/all_gather | solution.py:168
Sparse Core Ops, SparseCore 0:
  38.8 74.9 reduce-scatter.4
  116.1 70.6 reduce-scatter.2
  188.6 43.4 all-gather.6
  233.8 45.0 all-gather.4
